TPU v7x, 256 devices: a whole 4x4x8 slice. The times are simulated.
256 devices in a mesh: dp: 2 (over core), blk: 128 (over z, x, y).
Axes of the slice: x: 4, y: 4, z: 8, core: 2. Of those that a mesh axis runs over, the one named last changes fastest.
Arguments:
- features: bfloat16 [2, 65536, 128], P('dp', 'blk'), may hold values from -24 to 24
- tile_mask: int32 [2, 128], P('dp', 'blk'), may hold values 0 or 1
- w_first: bfloat16 [3456, 128], replicated, may hold values from -0.109375 to 0.109375
- w_second: bfloat16 [3456, 128], replicated, may hold values from -0.109375 to 0.109375
- cotangent: bfloat16 [2, 65536, 128], P('dp', 'blk'), may hold values from -6 to 6
Outputs:
- grad_first: float32 [3456, 128], replicated
- grad_second: float32 [3456, 128], replicated
- feature_grad: bfloat16 [2, 65536, 128], P('dp', 'blk')
All inputs are finite; a program needn't handle non-finite values. No bound on the sum of `tile_mask` on one device may be relied on, other than what follows from the above.
Results may differ from a plain program's by a relative error of at most 0.0039.
Values may be sent and summed in bfloat16 or wider, within the bound.
A program may use at most 64 MiB of HBM per device.

v0:
```python
import jax
import jax.numpy as jnp
from jax import lax
from jax.sharding import PartitionSpec as P

TILE = 8
unscale = 1.0 / 512.0


def shifted(value, axis, steps):
    count = lax.axis_size(axis)
    leading, last = (max(0, -steps), min(count, count - steps))
    return lax.ppermute(value, axis, [(source, source + steps) for source in range(leading, last)])


def stack_depth(padded, depth_z):
    return jnp.concatenate(
        [padded[:, :, shift_z : shift_z + depth_z, :] for shift_z in range(3)], axis=-1
    )


def arrange(weight):
    width_in = weight.shape[0] // 27
    width_out = weight.shape[1]
    shaped = weight.reshape(width_in, 3, 3, 3, width_out).transpose(1, 2, 3, 0, 4)
    return shaped.reshape(3, 3, 3 * width_in, width_out)


def arrange_flipped(weight):
    width_in = weight.shape[0] // 27
    width_out = weight.shape[1]
    shaped = weight.reshape(width_in, 3, 3, 3, width_out)[:, ::-1, ::-1, ::-1, :].transpose(
        1, 2, 3, 4, 0
    )
    return shaped.reshape(3, 3, 3 * width_out, width_in)


def convolve(padded, kernel):
    size_x = padded.shape[0] - 2
    size_y = padded.shape[1] - 2
    size_z = padded.shape[2] - 2
    stacked = stack_depth(padded, size_z)
    summed = jnp.zeros((size_x * size_y * size_z, kernel.shape[-1]), jnp.float32)
    for step_x in range(3):
        for step_y in range(3):
            slab_rows = stacked[step_x : step_x + size_x, step_y : step_y + size_y].reshape(
                -1, stacked.shape[-1]
            )
            summed = summed + jnp.dot(
                slab_rows, kernel[step_x, step_y], preferred_element_type=jnp.float32
            )
    return summed


def correlate(padded, grads):
    size_x = padded.shape[0] - 2
    size_y = padded.shape[1] - 2
    size_z = padded.shape[2] - 2
    width_in = padded.shape[3]
    width_out = grads.shape[1]
    stacked = stack_depth(padded, size_z)
    blocks = []
    for step_x in range(3):
        for step_y in range(3):
            slab_rows = stacked[step_x : step_x + size_x, step_y : step_y + size_y].reshape(
                -1, stacked.shape[-1]
            )
            blocks.append(
                lax.dot_general(
                    slab_rows, grads, (((0,), (0,)), ((), ())), preferred_element_type=jnp.float32
                )
            )
    joined = jnp.stack(blocks).reshape(3, 3, 3, width_in, width_out).transpose(3, 0, 1, 2, 4)
    return joined.reshape(27 * width_in, width_out)


def direct_rims(values, place, extent):
    padded = jnp.pad(values, ((1, 1), (1, 1), (1, 1), (0, 0)))
    for shift_x in (-1, 0, 1):
        for shift_y in (-1, 0, 1):
            for shift_z in (-1, 0, 1):
                moves = (shift_x, shift_y, shift_z)
                if moves == (0, 0, 0):
                    continue
                sliced = values
                inside = jnp.asarray(True)
                starts = []
                for axis_pos in range(3):
                    toward = moves[axis_pos]
                    length = values.shape[axis_pos]
                    if toward == 1:
                        sliced = lax.slice_in_dim(sliced, 0, 1, axis=axis_pos)
                        starts.append(length + 1)
                    elif toward == -1:
                        sliced = lax.slice_in_dim(sliced, length - 1, length, axis=axis_pos)
                        starts.append(0)
                    else:
                        starts.append(1)
                    inside = (
                        inside
                        & (place[axis_pos] + toward >= 0)
                        & (place[axis_pos] + toward < extent[axis_pos])
                    )
                offset = shift_x * 16 + shift_y * 4 + shift_z
                arrived = shifted(sliced, "blk", -offset)
                arrived = jnp.where(inside, arrived, jnp.zeros_like(arrived))
                padded = lax.dynamic_update_slice(
                    padded, arrived, (starts[0], starts[1], starts[2], 0)
                )
    return padded


def surround(values, place, extent):
    return direct_rims(values, place, extent)


def reduce_rows(term):
    return lax.psum(term, ("dp", "blk"))


def on_device(features, tile_mask, w_first, w_second, cotangent):
    width = features.shape[2]
    size_x = tile_mask.shape[1] * TILE
    region = (size_x, TILE, TILE, width)
    device_index = lax.axis_index("blk")
    place = (device_index // 16, device_index // 4 % 4, device_index % 4)
    extent = (lax.axis_size("blk") // 16, 4, 4)
    keep_rows = jnp.repeat(tile_mask[0], TILE * TILE * TILE).astype(jnp.bfloat16)[:, None]
    keep_float = keep_rows.astype(jnp.float32)
    inputs = features[0] * keep_rows
    grads_out = cotangent[0] * keep_rows
    pad_in = surround(inputs.reshape(region), place, extent)
    pre_act = convolve(pad_in, arrange(w_first))
    hidden = (jax.nn.silu(pre_act) * keep_float).astype(jnp.bfloat16)
    pad_hidden = surround(hidden.reshape(region), place, extent)
    pad_grads = surround(grads_out.reshape(region), place, extent)
    grad_second = reduce_rows(correlate(pad_hidden, grads_out) * unscale)
    back = convolve(pad_grads, arrange_flipped(w_second))
    sigma = jax.nn.sigmoid(pre_act)
    pre_grad = (back * sigma * (1.0 + pre_act * (1.0 - sigma)) * keep_float).astype(jnp.bfloat16)
    pad_pre = surround(pre_grad.reshape(region), place, extent)
    grad_first = reduce_rows(correlate(pad_in, pre_grad) * unscale)
    summed = grads_out.astype(jnp.float32) + convolve(pad_pre, arrange_flipped(w_first))
    result = (summed * keep_float).astype(jnp.bfloat16)
    return (grad_first, grad_second, result[None])


def solution(mesh):
    in_specs = (P("dp", "blk", None), P("dp", "blk"), P(), P(), P("dp", "blk", None))
    out_specs = (P(), P(), P("dp", "blk", None))
    return jax.shard_map(
        on_device, mesh=mesh, in_specs=in_specs, out_specs=out_specs, check_vma=False
    )
```

profile of v0, /device:TPU:97, one launch (start us, length us, event | category | flops | bytes accessed | tf_op | source)
XLA Modules:
  0.0 1220.6 jit_solution(1918076127340199430)
XLA Ops:
  14.3 7.1 collective-permute-start.8
  71.6 9.0 collective-permute-start.2
  81.3 6.9 collective-permute-start.28
  91.5 7.8 collective-permute-done
  101.2 7.8 collective-permute-done.26
  126.1 7.2 collective-permute-done.23
  159.1 8.3 collective-permute-done.17
  169.4 6.0 collective-permute-done.43
  218.5 6.1 collective-permute-done.35
  227.1 6.3 collective-permute-done.9
  233.5 8.0 collective-permute-start.5
  242.2 6.9 collective-permute-start.31
  249.9 8.9 collective-permute-start.3
  284.4 12.4 %collective-permute-done.20 = bf16[1,8,1,128]{3,2,1,0:T(2,128)(2,1)S(1)} collective-permute-done((bf16[1,8,1,128]{3,2,1,0:T(2,128)(2,1)S(1)}, bf16[1,8,1,128]{3,2,1,0:T(2,128)(2,1)S(1)}, u32[]{:S(2)}, u32[]{:S(2)}) %collective-permute-start.20) | collective-permute-done | bytes 2080 | tf_op jit(solution)/shard_map/ppermute | solution.py:13
  362.0 7.0 collective-permute-done.12
  400.1 6.3 collective-permute-done.38
  452.5 9.4 collective-permute-start.82
  490.7 6.3 collective-permute-done.80
  530.5 6.2 collective-permute-done.95
  549.4 6.2 collective-permute-start.54
  560.0 7.6 collective-permute-done.52
  619.5 6.5 collective-permute-done.61
  647.1 6.7 collective-permute-done.87
  653.8 8.9 collective-permute-start.83
  681.7 6.2 collective-permute-done.98
  696.2 7.7 collective-permute-done.55
  712.5 6.2 collective-permute-done.72
  749.7 8.7 collective-permute-start.53
  771.9 6.7 collective-permute-start.65
  781.6 7.2 collective-permute-done.64
  816.7 7.0 collective-permute-done.90
  840.7 368.9 %all-reduce.7.cloned.1.call-done = (f32[3456,128]{1,0:T(8,128)}, f32[3456,128]{1,0:T(8,128)}) async-done(((f32[3456,128]{1,0:T(8,128)}, f32[3456,128]{1,0:T(8,128)}), (f32[3456,128]{1,0:T(8,128)}, f32[3456,128]{1,0:T(8,128)})) %all-reduce.7.cloned.1.call-update) | async-done | bytes 3538960 | tf_op jit(solution)/shard_map/psum | solution.py:118
  (626 shorter events, 604.0 us)
Async XLA Ops:
  7.2 1202.4 %all-reduce.7.cloned.1.call-start = ((), (), s32[]{:S(2)}) async-start(), calls=%async_computation | async-start | bytes 7077888 | tf_op jit(solution)/shard_map/psum | solution.py:118
  8.9 376.5 %collective-permute-start.4 = (bf16[1,8,8,128]{3,2,1,0:T(8,128)(2,1)S(1)}, bf16[1,8,8,128]{3,2,1,0:T(8,128)(2,1)S(1)}, u32[]{:S(2)}, u32[]{:S(2)}) collective-permute-start(bf16[1,8,8,128]{3,2,1,0:T(8,128)(2,1)S(1)} %get-tuple-element.84), channel_id=1, source_target_pairs={{0,16},{1,17},{2,18},{3,19},{4,20},{5,21},{6,22},{7,23},{8,24},{9,... | collective-permute-start | bytes 49160 | tf_op jit(solution)/shard_map/ppermute | solution.py:13
  14.3 38.4 %collective-permute-start.8 = (bf16[1,1,1,128]{3,2,1,0:T(2,128)(2,1)}, bf16[1,1,1,128]{3,2,1,0:T(2,128)(2,1)}, u32[]{:S(2)}, u32[]{:S(2)}) collective-permute-start(bf16[1,1,1,128]{3,2,1,0:T(2,128)(2,1)} %get-tuple-element.149), channel_id=1, source_target_pairs={{0,11},{1,12},{2,13},{3,14},{4,15},{5,16},{6,17},{7,18},{8,19},{9,... | collective-permute-start | bytes 776 | tf_op jit(solution)/shard_map/ppermute | solution.py:13
  21.4 367.4 %collective-permute-start.21 = (bf16[1,8,8,128]{3,2,1,0:T(8,128)(2,1)S(1)}, bf16[1,8,8,128]{3,2,1,0:T(8,128)(2,1)S(1)}, u32[]{:S(2)}, u32[]{:S(2)}) collective-permute-start(bf16[1,8,8,128]{3,2,1,0:T(8,128)(2,1)S(1)} %get-tuple-element.83), channel_id=1, source_target_pairs={{16,0},{17,1},{18,2},{19,3},{20,4},{21,5},{22,6},{23,7},{24,8},{25... | collective-permute-start | bytes 49160 | tf_op jit(solution)/shard_map/ppermute | solution.py:13
  23.4 408.3 %collective-permute-start.47 = (bf16[1,8,8,128]{3,2,1,0:T(8,128)(2,1)S(1)}, bf16[1,8,8,128]{3,2,1,0:T(8,128)(2,1)S(1)}, u32[]{:S(2)}, u32[]{:S(2)}) collective-permute-start(bf16[1,8,8,128]{3,2,1,0:T(8,128)(2,1)S(1)} %get-tuple-element.73), channel_id=1, source_target_pairs={{16,0},{17,1},{18,2},{19,3},{20,4},{21,5},{22,6},{23,7},{24,8},{25... | collective-permute-start | bytes 49160 | tf_op jit(solution)/shard_map/ppermute | solution.py:13
  25.3 382.5 %collective-permute-start.30 = (bf16[1,8,8,128]{3,2,1,0:T(8,128)(2,1)S(1)}, bf16[1,8,8,128]{3,2,1,0:T(8,128)(2,1)}, u32[]{:S(2)}, u32[]{:S(2)}) collective-permute-start(bf16[1,8,8,128]{3,2,1,0:T(8,128)(2,1)S(1)} %get-tuple-element.74), channel_id=1, source_target_pairs={{0,16},{1,17},{2,18},{3,19},{4,20},{5,21},{6,22},{7,23},{8,24},{9,... | collective-permute-start | bytes 49160 | tf_op jit(solution)/shard_map/ppermute | solution.py:13
  71.6 9.7 collective-permute-start.2
  89.5 9.7 collective-permute-start
  99.3 9.7 collective-permute-start.26
  123.6 9.7 collective-permute-start.23
  155.4 12.0 collective-permute-start.17
  249.9 9.6 collective-permute-start.3
  259.5 9.5 collective-permute-start.29
  281.9 14.9 %collective-permute-start.20 = (bf16[1,8,1,128]{3,2,1,0:T(2,128)(2,1)S(1)}, bf16[1,8,1,128]{3,2,1,0:T(2,128)(2,1)S(1)}, u32[]{:S(2)}, u32[]{:S(2)}) collective-permute-start(bf16[1,8,1,128]{3,2,1,0:T(2,128)(2,1)S(1)} %get-tuple-element.148), channel_id=1, source_target_pairs={{15,0},{16,1},{17,2},{18,3},{19,4},{20,5},{21,6},{22,7},{23,8},{24... | collective-permute-start | bytes 6152 | tf_op jit(solution)/shard_map/ppermute | solution.py:13
  360.0 9.0 collective-permute-start.12
  382.0 25.0 %collective-permute-start.41 = (bf16[8,1,8,128]{3,2,1,0:T(8,128)(2,1)}, bf16[8,1,8,128]{3,2,1,0:T(8,128)(2,1)}, u32[]{:S(2)}, u32[]{:S(2)}) collective-permute-start(bf16[8,1,8,128]{3,2,1,0:T(8,128)(2,1)} %get-tuple-element.79), channel_id=1, source_target_pairs={{4,0},{5,1},{6,2},{7,3},{8,4},{9,5},{10,6},{11,7},{12,8},{13,9},{1... | collective-permute-start | bytes 49160 | tf_op jit(solution)/shard_map/ppermute | solution.py:13
  385.4 22.4 %collective-permute-start.36 = (bf16[8,1,8,128]{3,2,1,0:T(8,128)(2,1)}, bf16[8,1,8,128]{3,2,1,0:T(8,128)(2,1)}, u32[]{:S(2)}, u32[]{:S(2)}) collective-permute-start(bf16[8,1,8,128]{3,2,1,0:T(8,128)(2,1)} %get-tuple-element.80), channel_id=1, source_target_pairs={{0,4},{1,5},{2,6},{3,7},{4,8},{5,9},{6,10},{7,11},{8,12},{9,13},{1... | collective-permute-start | bytes 49160 | tf_op jit(solution)/shard_map/ppermute | solution.py:13
  397.3 9.1 collective-permute-start.38
  448.3 377.5 %collective-permute-start.99 = (bf16[1,8,8,128]{3,2,1,0:T(8,128)(2,1)S(1)}, bf16[1,8,8,128]{3,2,1,0:T(8,128)(2,1)S(1)}, u32[]{:S(2)}, u32[]{:S(2)}) collective-permute-start(bf16[1,8,8,128]{3,2,1,0:T(8,128)(2,1)S(1)} %get-tuple-element.53), channel_id=1, source_target_pairs={{16,0},{17,1},{18,2},{19,3},{20,4},{21,5},{22,6},{23,7},{24,8},{25... | collective-permute-start | bytes 49160 | tf_op jit(solution)/shard_map/ppermute | solution.py:13
  452.5 371.2 %collective-permute-start.82 = (bf16[1,8,8,128]{3,2,1,0:T(8,128)(2,1)S(1)}, bf16[1,8,8,128]{3,2,1,0:T(8,128)(2,1)}, u32[]{:S(2)}, u32[]{:S(2)}) collective-permute-start(bf16[1,8,8,128]{3,2,1,0:T(8,128)(2,1)S(1)} %get-tuple-element.54), channel_id=1, source_target_pairs={{0,16},{1,17},{2,18},{3,19},{4,20},{5,21},{6,22},{7,23},{8,24},{9,... | collective-permute-start | bytes 49160 | tf_op jit(solution)/shard_map/ppermute | solution.py:13
  465.5 343.6 %collective-permute-start.73 = (bf16[1,8,8,128]{3,2,1,0:T(8,128)(2,1)S(1)}, bf16[1,8,8,128]{3,2,1,0:T(8,128)(2,1)}, u32[]{:S(2)}, u32[]{:S(2)}) collective-permute-start(bf16[1,8,8,128]{3,2,1,0:T(8,128)(2,1)S(1)} %get-tuple-element.63), channel_id=1, source_target_pairs={{16,0},{17,1},{18,2},{19,3},{20,4},{21,5},{22,6},{23,7},{24,8},{25... | collective-permute-start | bytes 49160 | tf_op jit(solution)/shard_map/ppermute | solution.py:13
  467.4 337.4 %collective-permute-start.56 = (bf16[1,8,8,128]{3,2,1,0:T(8,128)(2,1)S(1)}, bf16[1,8,8,128]{3,2,1,0:T(8,128)(2,1)}, u32[]{:S(2)}, u32[]{:S(2)}) collective-permute-start(bf16[1,8,8,128]{3,2,1,0:T(8,128)(2,1)S(1)} %get-tuple-element.64), channel_id=1, source_target_pairs={{0,16},{1,17},{2,18},{3,19},{4,20},{5,21},{6,22},{7,23},{8,24},{9,... | collective-permute-start | bytes 49160 | tf_op jit(solution)/shard_map/ppermute | solution.py:13
  497.0 9.7 collective-permute-start.78
  557.7 9.9 collective-permute-start.52
  644.8 9.1 collective-permute-start.87
  653.8 9.6 collective-permute-start.83
  663.4 9.7 collective-permute-start.81
  694.3 9.7 collective-permute-start.55
  749.7 9.6 collective-permute-start.53
  779.7 9.2 collective-permute-start.64
  801.4 22.2 %collective-permute-start.93 = (bf16[8,1,8,128]{3,2,1,0:T(8,128)(2,1)}, bf16[8,1,8,128]{3,2,1,0:T(8,128)(2,1)S(1)}, u32[]{:S(2)}, u32[]{:S(2)}) collective-permute-start(bf16[8,1,8,128]{3,2,1,0:T(8,128)(2,1)} %get-tuple-element.59), channel_id=1, source_target_pairs={{4,0},{5,1},{6,2},{7,3},{8,4},{9,5},{10,6},{11,7},{12,8},{13,9},{1... | collective-permute-start | bytes 49160 | tf_op jit(solution)/shard_map/ppermute | solution.py:13
  804.8 18.9 %collective-permute-start.88 = (bf16[8,1,8,128]{3,2,1,0:T(8,128)(2,1)}, bf16[8,1,8,128]{3,2,1,0:T(8,128)(2,1)S(1)}, u32[]{:S(2)}, u32[]{:S(2)}) collective-permute-start(bf16[8,1,8,128]{3,2,1,0:T(8,128)(2,1)} %get-tuple-element.60), channel_id=1, source_target_pairs={{0,4},{1,5},{2,6},{3,7},{4,8},{5,9},{6,10},{7,11},{8,12},{9,13},{1... | collective-permute-start | bytes 49160 | tf_op jit(solution)/shard_map/ppermute | solution.py:13
  (134 other events, 7441.9 us)
Sparse Core Ops, SparseCore 0:
  836.7 372.8 all-reduce.6
where the time goes:
time: 1230 us; the launch traced here: 1220 us
  waiting for transfers between devices  736 us (60%)
  starting transfers between devices  346 us (28%)
  local copies, waits for them, and re-layouts  88.6 us (7%)
  between operations  18 us (1%)
  other arithmetic  16.7 us (1%)
  matrix products  15.1 us (1%)
    psum x1, waiting for transfers between devices, reduce_rows(): return lax.psum(term, ('dp', 'blk'))  369 us
    ppermute x104, waiting for transfers between devices, shifted(): lax.ppermute(value, axis, [(source, source + steps) for source in range(l...  367 us
    ppermute x104, starting transfers between devices, shifted(): lax.ppermute(value, axis, [(source, source + steps) for source in range(l...  346 us
    dynamic_update_slice x104, local copies, waits for them, and re-layouts, direct_rims(): lax.dynamic_update_slice(padded, arrived, (starts[0], starts[1], starts[2...  35.9 us
  transfers between devices with their start and end apart: 105, of which 89 were waited for; matrix products, arithmetic and copies ran while one was open for 7% of the time, Pallas kernels for 0%

commit v1 on v0

--- a/solution.py
+++ b/solution.py
@@ -115,7 +115,7 @@
 
 
 def reduce_rows(term):
-    return lax.psum(term, ("dp", "blk"))
+    return lax.psum(lax.psum(term, "blk"), "dp")
 
 
 def on_device(features, tile_mask, w_first, w_second, cotangent):

time: 1230 us -> 1090 us (0.89)
  waiting for transfers between devices: 736 us -> 602 us
    psum x1 -> x2, waiting for transfers between devices: 369 us -> 253 us  [reduce_rows(): return lax.psum(lax.psum(term, 'blk'), 'dp')]
    ppermute x104, waiting for transfers between devices: 367 us -> 350 us  [shifted(): lax.ppermute(value, axis, [(source, source + steps) for source in range(l...]
  transfers between devices with their start and end apart: 105 -> 106, of which waited for: 89 -> 86; matrix products, arithmetic and copies ran while one was open for 7% -> 9% of each run, Pallas kernels for 0% -> 0%
where the time goes in v1:
time: 1090 us; the launch traced here: 1080 us
  waiting for transfers between devices  602 us (55%)
  starting transfers between devices  344 us (32%)
  local copies, waits for them, and re-layouts  87.4 us (8%)
  between operations  18 us (2%)
  other arithmetic  16.6 us (2%)
  matrix products  14.2 us (1%)
    ppermute x104, waiting for transfers between devices, shifted(): lax.ppermute(value, axis, [(source, source + steps) for source in range(l...  350 us
    ppermute x104, starting transfers between devices, shifted(): lax.ppermute(value, axis, [(source, source + steps) for source in range(l...  344 us
    psum x2, waiting for transfers between devices, reduce_rows(): return lax.psum(lax.psum(term, 'blk'), 'dp')  253 us
    dynamic_update_slice x104, local copies, waits for them, and re-layouts, direct_rims(): lax.dynamic_update_slice(padded, arrived, (starts[0], starts[1], starts[2...  36 us
  transfers between devices with their start and end apart: 106, of which 86 were waited for; matrix products, arithmetic and copies ran while one was open for 9% of the time, Pallas kernels for 0%

profile of v1, /device:TPU:97, one launch (start us, length us, event | category | flops | bytes accessed | tf_op | source)
XLA Modules:
  0.0 1082.4 jit_solution(9512443539582717492)
XLA Ops:
  14.3 7.1 collective-permute-start.8
  71.7 9.0 collective-permute-start.2
  81.4 6.9 collective-permute-start.28
  91.5 7.8 collective-permute-done
  101.2 7.8 collective-permute-done.26
  126.1 7.2 collective-permute-done.23
  159.2 8.3 collective-permute-done.17
  169.4 6.0 collective-permute-done.43
  218.5 6.1 collective-permute-done.35
  227.1 6.3 collective-permute-done.9
  233.5 8.0 collective-permute-start.5
  242.2 6.9 collective-permute-start.31
  249.9 8.9 collective-permute-start.3
  284.4 12.4 %collective-permute-done.20 = bf16[1,8,1,128]{3,2,1,0:T(2,128)(2,1)S(1)} collective-permute-done((bf16[1,8,1,128]{3,2,1,0:T(2,128)(2,1)S(1)}, bf16[1,8,1,128]{3,2,1,0:T(2,128)(2,1)S(1)}, u32[]{:S(2)}, u32[]{:S(2)}) %collective-permute-start.20) | collective-permute-done | bytes 2080 | tf_op jit(solution)/shard_map/ppermute | solution.py:13
  362.0 7.0 collective-permute-done.12
  400.1 6.3 collective-permute-done.38
  452.7 9.4 collective-permute-start.82
  490.9 6.3 collective-permute-done.80
  534.9 6.5 collective-permute-start.54
  545.1 8.0 collective-permute-done.52
  562.4 6.3 collective-permute-done.75
  605.6 6.2 collective-permute-done.61
  617.5 8.1 collective-permute-start.55
  635.6 7.1 collective-permute-done.72
  668.3 6.9 collective-permute-start.65
  678.2 7.2 collective-permute-done.64
  726.5 6.1 collective-permute-start.87
  738.0 10.2 collective-permute-start.83
  750.9 7.5 collective-permute-done.81
  804.3 7.2 collective-permute-done.90
  811.5 218.5 %all-reduce.9.cloned.1.call-done = (f32[3456,128]{1,0:T(8,128)}, f32[3456,128]{1,0:T(8,128)}) async-done(((f32[3456,128]{1,0:T(8,128)}, f32[3456,128]{1,0:T(8,128)}), (f32[3456,128]{1,0:T(8,128)}, f32[3456,128]{1,0:T(8,128)})) %all-reduce.9.cloned.1.call-update) | async-done | bytes 3538960 | tf_op jit(solution)/shard_map/psum | solution.py:118
  1037.2 34.3 %all-reduce.11.cloned.1.call-done = (f32[3456,128]{1,0:T(8,128)}, f32[3456,128]{1,0:T(8,128)}) async-done(((f32[3456,128]{1,0:T(8,128)}, f32[3456,128]{1,0:T(8,128)}), (f32[3456,128]{1,0:T(8,128)}, f32[3456,128]{1,0:T(8,128)})) %all-reduce.11.cloned.1.call-update) | async-done | bytes 3538960 | tf_op jit(solution)/shard_map/psum | solution.py:118
  (639 shorter events, 586.5 us)
Async XLA Ops:
  7.2 1022.9 %all-reduce.9.cloned.1.call-start = ((), (), s32[]{:S(2)}) async-start(), calls=%async_computation | async-start | bytes 7077888 | tf_op jit(solution)/shard_map/psum | solution.py:118
  8.9 376.5 %collective-permute-start.4 = (bf16[1,8,8,128]{3,2,1,0:T(8,128)(2,1)S(1)}, bf16[1,8,8,128]{3,2,1,0:T(8,128)(2,1)S(1)}, u32[]{:S(2)}, u32[]{:S(2)}) collective-permute-start(bf16[1,8,8,128]{3,2,1,0:T(8,128)(2,1)S(1)} %get-tuple-element.86), channel_id=1, source_target_pairs={{0,16},{1,17},{2,18},{3,19},{4,20},{5,21},{6,22},{7,23},{8,24},{9,... | collective-permute-start | bytes 49160 | tf_op jit(solution)/shard_map/ppermute | solution.py:13
  14.3 38.4 %collective-permute-start.8 = (bf16[1,1,1,128]{3,2,1,0:T(2,128)(2,1)}, bf16[1,1,1,128]{3,2,1,0:T(2,128)(2,1)}, u32[]{:S(2)}, u32[]{:S(2)}) collective-permute-start(bf16[1,1,1,128]{3,2,1,0:T(2,128)(2,1)} %get-tuple-element.151), channel_id=1, source_target_pairs={{0,11},{1,12},{2,13},{3,14},{4,15},{5,16},{6,17},{7,18},{8,19},{9,... | collective-permute-start | bytes 776 | tf_op jit(solution)/shard_map/ppermute | solution.py:13
  21.4 367.4 %collective-permute-start.21 = (bf16[1,8,8,128]{3,2,1,0:T(8,128)(2,1)S(1)}, bf16[1,8,8,128]{3,2,1,0:T(8,128)(2,1)S(1)}, u32[]{:S(2)}, u32[]{:S(2)}) collective-permute-start(bf16[1,8,8,128]{3,2,1,0:T(8,128)(2,1)S(1)} %get-tuple-element.85), channel_id=1, source_target_pairs={{16,0},{17,1},{18,2},{19,3},{20,4},{21,5},{22,6},{23,7},{24,8},{25... | collective-permute-start | bytes 49160 | tf_op jit(solution)/shard_map/ppermute | solution.py:13
  23.3 408.5 %collective-permute-start.47 = (bf16[1,8,8,128]{3,2,1,0:T(8,128)(2,1)S(1)}, bf16[1,8,8,128]{3,2,1,0:T(8,128)(2,1)S(1)}, u32[]{:S(2)}, u32[]{:S(2)}) collective-permute-start(bf16[1,8,8,128]{3,2,1,0:T(8,128)(2,1)S(1)} %get-tuple-element.75), channel_id=1, source_target_pairs={{16,0},{17,1},{18,2},{19,3},{20,4},{21,5},{22,6},{23,7},{24,8},{25... | collective-permute-start | bytes 49160 | tf_op jit(solution)/shard_map/ppermute | solution.py:13
  25.3 382.6 %collective-permute-start.30 = (bf16[1,8,8,128]{3,2,1,0:T(8,128)(2,1)S(1)}, bf16[1,8,8,128]{3,2,1,0:T(8,128)(2,1)}, u32[]{:S(2)}, u32[]{:S(2)}) collective-permute-start(bf16[1,8,8,128]{3,2,1,0:T(8,128)(2,1)S(1)} %get-tuple-element.76), channel_id=1, source_target_pairs={{0,16},{1,17},{2,18},{3,19},{4,20},{5,21},{6,22},{7,23},{8,24},{9,... | collective-permute-start | bytes 49160 | tf_op jit(solution)/shard_map/ppermute | solution.py:13
  71.7 9.7 collective-permute-start.2
  89.6 9.7 collective-permute-start
  99.3 9.7 collective-permute-start.26
  123.6 9.7 collective-permute-start.23
  155.4 12.0 %collective-permute-start.17 = (bf16[1,1,1,128]{3,2,1,0:T(2,128)(2,1)S(1)}, bf16[1,1,1,128]{3,2,1,0:T(2,128)(2,1)S(1)}, u32[]{:S(2)}, u32[]{:S(2)}) collective-permute-start(bf16[1,1,1,128]{3,2,1,0:T(2,128)(2,1)S(1)} %copy-done.51), channel_id=1, source_target_pairs={{11,0},{12,1},{13,2},{14,3},{15,4},{16,5},{17,6},{18,7},{19,8},{20... | collective-permute-start | bytes 776 | tf_op jit(solution)/shard_map/ppermute | solution.py:13
  249.9 9.6 collective-permute-start.3
  259.5 9.5 collective-permute-start.29
  281.9 14.9 %collective-permute-start.20 = (bf16[1,8,1,128]{3,2,1,0:T(2,128)(2,1)S(1)}, bf16[1,8,1,128]{3,2,1,0:T(2,128)(2,1)S(1)}, u32[]{:S(2)}, u32[]{:S(2)}) collective-permute-start(bf16[1,8,1,128]{3,2,1,0:T(2,128)(2,1)S(1)} %get-tuple-element.150), channel_id=1, source_target_pairs={{15,0},{16,1},{17,2},{18,3},{19,4},{20,5},{21,6},{22,7},{23,8},{24... | collective-permute-start | bytes 6152 | tf_op jit(solution)/shard_map/ppermute | solution.py:13
  382.1 25.0 %collective-permute-start.41 = (bf16[8,1,8,128]{3,2,1,0:T(8,128)(2,1)}, bf16[8,1,8,128]{3,2,1,0:T(8,128)(2,1)}, u32[]{:S(2)}, u32[]{:S(2)}) collective-permute-start(bf16[8,1,8,128]{3,2,1,0:T(8,128)(2,1)} %get-tuple-element.81), channel_id=1, source_target_pairs={{4,0},{5,1},{6,2},{7,3},{8,4},{9,5},{10,6},{11,7},{12,8},{13,9},{1... | collective-permute-start | bytes 49160 | tf_op jit(solution)/shard_map/ppermute | solution.py:13
  385.4 22.4 %collective-permute-start.36 = (bf16[8,1,8,128]{3,2,1,0:T(8,128)(2,1)}, bf16[8,1,8,128]{3,2,1,0:T(8,128)(2,1)}, u32[]{:S(2)}, u32[]{:S(2)}) collective-permute-start(bf16[8,1,8,128]{3,2,1,0:T(8,128)(2,1)} %get-tuple-element.82), channel_id=1, source_target_pairs={{0,4},{1,5},{2,6},{3,7},{4,8},{5,9},{6,10},{7,11},{8,12},{9,13},{1... | collective-permute-start | bytes 49160 | tf_op jit(solution)/shard_map/ppermute | solution.py:13
  448.5 583.8 %collective-permute-start.99 = (bf16[1,8,8,128]{3,2,1,0:T(8,128)(2,1)S(1)}, bf16[1,8,8,128]{3,2,1,0:T(8,128)(2,1)S(1)}, u32[]{:S(2)}, u32[]{:S(2)}) collective-permute-start(bf16[1,8,8,128]{3,2,1,0:T(8,128)(2,1)S(1)} %get-tuple-element.55), channel_id=1, source_target_pairs={{16,0},{17,1},{18,2},{19,3},{20,4},{21,5},{22,6},{23,7},{24,8},{25... | collective-permute-start | bytes 49160 | tf_op jit(solution)/shard_map/ppermute | solution.py:13
  452.7 577.4 %collective-permute-start.82 = (bf16[1,8,8,128]{3,2,1,0:T(8,128)(2,1)S(1)}, bf16[1,8,8,128]{3,2,1,0:T(8,128)(2,1)}, u32[]{:S(2)}, u32[]{:S(2)}) collective-permute-start(bf16[1,8,8,128]{3,2,1,0:T(8,128)(2,1)S(1)} %get-tuple-element.56), channel_id=1, source_target_pairs={{0,16},{1,17},{2,18},{3,19},{4,20},{5,21},{6,22},{7,23},{8,24},{9,... | collective-permute-start | bytes 49160 | tf_op jit(solution)/shard_map/ppermute | solution.py:13
  465.7 238.3 %collective-permute-start.73 = (bf16[1,8,8,128]{3,2,1,0:T(8,128)(2,1)S(1)}, bf16[1,8,8,128]{3,2,1,0:T(8,128)(2,1)}, u32[]{:S(2)}, u32[]{:S(2)}) collective-permute-start(bf16[1,8,8,128]{3,2,1,0:T(8,128)(2,1)S(1)} %get-tuple-element.65), channel_id=1, source_target_pairs={{16,0},{17,1},{18,2},{19,3},{20,4},{21,5},{22,6},{23,7},{24,8},{25... | collective-permute-start | bytes 49160 | tf_op jit(solution)/shard_map/ppermute | solution.py:13
  467.6 232.3 %collective-permute-start.56 = (bf16[1,8,8,128]{3,2,1,0:T(8,128)(2,1)S(1)}, bf16[1,8,8,128]{3,2,1,0:T(8,128)(2,1)}, u32[]{:S(2)}, u32[]{:S(2)}) collective-permute-start(bf16[1,8,8,128]{3,2,1,0:T(8,128)(2,1)S(1)} %get-tuple-element.66), channel_id=1, source_target_pairs={{0,16},{1,17},{2,18},{3,19},{4,20},{5,21},{6,22},{7,23},{8,24},{9,... | collective-permute-start | bytes 49160 | tf_op jit(solution)/shard_map/ppermute | solution.py:13
  497.2 9.8 collective-permute-start.78
  543.2 9.9 collective-permute-start.52
  617.5 9.5 collective-permute-start.55
  696.8 29.7 %collective-permute-start.94 = (bf16[8,1,1,128]{3,2,1,0:T(2,128)(2,1)}, bf16[8,1,1,128]{3,2,1,0:T(2,128)(2,1)S(1)}, u32[]{:S(2)}, u32[]{:S(2)}) collective-permute-start(bf16[8,1,1,128]{3,2,1,0:T(2,128)(2,1)} %get-tuple-element.57), channel_id=1, source_target_pairs={{5,0},{6,1},{7,2},{8,3},{9,4},{10,5},{11,6},{12,7},{13,8},{14,9},{... | collective-permute-start | bytes 6152 | tf_op jit(solution)/shard_map/ppermute | solution.py:13
  700.0 32.7 %collective-permute-start.92 = (bf16[8,1,1,128]{3,2,1,0:T(2,128)(2,1)}, bf16[8,1,1,128]{3,2,1,0:T(2,128)(2,1)S(1)}, u32[]{:S(2)}, u32[]{:S(2)}) collective-permute-start(bf16[8,1,1,128]{3,2,1,0:T(2,128)(2,1)} %get-tuple-element.58), channel_id=1, source_target_pairs={{3,0},{4,1},{5,2},{6,3},{7,4},{8,5},{9,6},{10,7},{11,8},{12,9},{13... | collective-permute-start | bytes 6152 | tf_op jit(solution)/shard_map/ppermute | solution.py:13
  704.0 12.1 %collective-permute-start.97 = (bf16[1,1,1,128]{3,2,1,0:T(2,128)(2,1)}, bf16[1,1,1,128]{3,2,1,0:T(2,128)(2,1)S(1)}, u32[]{:S(2)}, u32[]{:S(2)}) collective-permute-start(bf16[1,1,1,128]{3,2,1,0:T(2,128)(2,1)} %get-tuple-element.97), channel_id=1, source_target_pairs={{13,0},{14,1},{15,2},{16,3},{17,4},{18,5},{19,6},{20,7},{21,8},{22... | collective-permute-start | bytes 776 | tf_op jit(solution)/shard_map/ppermute | solution.py:13
  716.1 355.3 %all-reduce.11.cloned.1.call-start = ((), (), s32[]{:S(2)}) async-start(), calls=%async_computation.1 | async-start | bytes 7077888 | tf_op jit(solution)/shard_map/psum | solution.py:118
  724.6 11.0 %collective-permute-start.89 = (bf16[8,1,1,128]{3,2,1,0:T(2,128)(2,1)S(1)}, bf16[8,1,1,128]{3,2,1,0:T(2,128)(2,1)S(1)}, u32[]{:S(2)}, u32[]{:S(2)}) collective-permute-start(bf16[8,1,1,128]{3,2,1,0:T(2,128)(2,1)S(1)} %copy-done.25), channel_id=1, source_target_pairs={{0,3},{1,4},{2,5},{3,6},{4,7},{5,8},{6,9},{7,10},{8,11},{9,12},{10... | collective-permute-start | bytes 6152 | tf_op jit(solution)/shard_map/ppermute | solution.py:13
  726.5 11.5 %collective-permute-start.87 = (bf16[8,1,1,128]{3,2,1,0:T(2,128)(2,1)S(1)}, bf16[8,1,1,128]{3,2,1,0:T(2,128)(2,1)S(1)}, u32[]{:S(2)}, u32[]{:S(2)}) collective-permute-start(bf16[8,1,1,128]{3,2,1,0:T(2,128)(2,1)S(1)} %copy-done.24), channel_id=1, source_target_pairs={{0,5},{1,6},{2,7},{3,8},{4,9},{5,10},{6,11},{7,12},{8,13},{9,14},{... | collective-permute-start | bytes 6152 | tf_op jit(solution)/shard_map/ppermute | solution.py:13
  732.7 297.4 %collective-permute-start.93 = (bf16[8,1,8,128]{3,2,1,0:T(8,128)(2,1)S(1)}, bf16[8,1,8,128]{3,2,1,0:T(8,128)(2,1)S(1)}, u32[]{:S(2)}, u32[]{:S(2)}) collective-permute-start(bf16[8,1,8,128]{3,2,1,0:T(8,128)(2,1)S(1)} %copy-done.12), channel_id=1, source_target_pairs={{4,0},{5,1},{6,2},{7,3},{8,4},{9,5},{10,6},{11,7},{12,8},{13,9},{1... | collective-permute-start | bytes 49160 | tf_op jit(solution)/shard_map/ppermute | solution.py:13
  735.6 294.6 %collective-permute-start.88 = (bf16[8,1,8,128]{3,2,1,0:T(8,128)(2,1)S(1)}, bf16[8,1,8,128]{3,2,1,0:T(8,128)(2,1)S(1)}, u32[]{:S(2)}, u32[]{:S(2)}) collective-permute-start(bf16[8,1,8,128]{3,2,1,0:T(8,128)(2,1)S(1)} %copy-done.11), channel_id=1, source_target_pairs={{0,4},{1,5},{2,6},{3,7},{4,8},{5,9},{6,10},{7,11},{8,12},{9,13},{1... | collective-permute-start | bytes 49160 | tf_op jit(solution)/shard_map/ppermute | solution.py:13
  738.0 10.9 %collective-permute-start.83 = (bf16[1,8,1,128]{3,2,1,0:T(2,128)(2,1)S(1)}, bf16[1,8,1,128]{3,2,1,0:T(2,128)(2,1)S(1)}, u32[]{:S(2)}, u32[]{:S(2)}) collective-permute-start(bf16[1,8,1,128]{3,2,1,0:T(2,128)(2,1)S(1)} %copy-done.18), channel_id=1, source_target_pairs={{0,15},{1,16},{2,17},{3,18},{4,19},{5,20},{6,21},{7,22},{8,23},{9,... | collective-permute-start | bytes 6152 | tf_op jit(solution)/shard_map/ppermute | solution.py:13
  (140 other events, 7574.6 us)
Sparse Core Ops, SparseCore 0:
  716.2 313.7 all-reduce.8
  1032.7 38.6 all-reduce.10
